TPU v7x, 128 devices: a whole 4x4x4 slice. The times are simulated.
128 devices in a mesh: req: 8 (over z, core), unit: 16 (over x, y).
Axes of the slice: x: 4, y: 4, z: 4, core: 2. Of those that a mesh axis runs over, the one named last changes fastest.
Arguments:
- tokens: bfloat16 [128, 384, 1536], P('req'), may hold values from -6 to 6
- lengths: int32 [128], P('req'), may hold values from 1 to 384, 30720 in all
- gate_proj: float32 [1536, 3072], P(('req', 'unit')), may hold values from -0.15625 to 0.15625
- input_proj: float32 [1536, 3072], P(('req', 'unit')), may hold values from -0.15625 to 0.15625
- state_proj: float32 [1536, 256], P(('req', 'unit')), may hold values from -0.15625 to 0.15625
- step_proj: float32 [1536, 48], P(('req', 'unit')), may hold values from -0.15625 to 0.15625
- out_proj: float32 [1536, 3072], P(('req', 'unit')), may hold values from -0.109375 to 0.109375
- conv_weight: float32 [4, 3328], replicated, may hold values from -3 to 3
- step_bias: float32 [48], replicated, may hold values from -4 to -1
- log_rate: float32 [48], replicated, may hold values from -3.5 to 0
- skip_gain: float32 [48], replicated, may hold values from 0.5 to 3
- norm_gain: float32 [3072], replicated, may hold values from 0.1 to 1.9
Outputs:
- mixed: bfloat16 [128, 384, 1536], P(('req', 'unit'))
- final_state: float32 [128, 48, 64, 128], P(('req', 'unit'))
All inputs are finite; a program needn't handle non-finite values. No bound on the sum of `lengths` on one device may be relied on, other than what follows from the above.
Results may differ from a plain program's by a relative error of at most 0.0084.
Values may be sent and summed in bfloat16 or wider, within the bound.
No kernel may reach another device: no remote copies, remote signals or barrier semaphores. Data moves between devices by JAX's collectives and lax.ppermute only.
A program may use at most 192 MiB of HBM per device.

v0:
```python
import jax
import jax.numpy as jnp
from jax import lax
from jax.sharding import PartitionSpec as P

SPAN = 128
EPSILON = 1e-05
HIGHEST = lax.Precision.HIGHEST


def causal_conv(values, kernel):
    kernel_len = kernel.shape[0]
    seq_len = values.shape[-2]
    axis_time = values.ndim - 2
    padding = [(0, 0)] * axis_time + [(kernel_len - 1, 0), (0, 0)]
    padded = jnp.pad(values.astype(jnp.float32), padding)
    running = jnp.zeros(values.shape, jnp.float32)
    for offset in range(kernel_len):
        running = running + kernel[offset] * lax.slice_in_dim(
            padded, offset, offset + seq_len, axis=axis_time
        )
    return jax.nn.silu(running)


def ssd_scan(head_in, step_size, b_matrix, c_matrix, rate_per, skip_gain, block_len):
    req_count, seq_len, head_count, head_dim = head_in.shape
    state_dim = b_matrix.shape[-1]
    blocks = seq_len // block_len
    b_short = b_matrix.astype(jnp.bfloat16)
    c_short = c_matrix.astype(jnp.bfloat16)
    b_wide = lax.optimization_barrier(b_short).astype(jnp.float32)
    c_wide = lax.optimization_barrier(c_short).astype(jnp.float32)
    shaped_x = jnp.moveaxis(
        head_in.reshape(req_count, blocks, block_len, head_count, head_dim), 1, 0
    )
    shaped_dt = jnp.moveaxis(step_size.reshape(req_count, blocks, block_len, head_count), 1, 0)
    shaped_bs = jnp.moveaxis(b_short.reshape(req_count, blocks, block_len, state_dim), 1, 0)
    shaped_cs = jnp.moveaxis(c_short.reshape(req_count, blocks, block_len, state_dim), 1, 0)
    shaped_b = jnp.moveaxis(b_wide.reshape(req_count, blocks, block_len, state_dim), 1, 0)
    shaped_c = jnp.moveaxis(c_wide.reshape(req_count, blocks, block_len, state_dim), 1, 0)
    decays = jnp.cumsum(shaped_dt * rate_per, axis=2)
    where_lower = jnp.arange(block_len)[:, None] >= jnp.arange(block_len)[None, :]

    def advance(carried, pieces):
        piece_x, piece_dt, piece_bs, piece_cs, piece_b, piece_c, piece_log = pieces
        intersection = jnp.einsum(
            "rtn,rsn->rts", piece_cs, piece_bs, preferred_element_type=jnp.float32
        )
        log_gaps = piece_log[:, :, None, :] - piece_log[:, None, :, :]
        factor = jnp.exp(jnp.where(where_lower[None, :, :, None], log_gaps, -jnp.inf))
        mixing = intersection[..., None] * factor * piece_dt[:, None, :, :]
        inside = jnp.einsum("rtsh,rshp->rthp", mixing, piece_x, precision=HIGHEST)
        earlier = (
            jnp.einsum("rtn,rhpn->rthp", piece_c, carried, precision=HIGHEST)
            * jnp.exp(piece_log)[..., None]
        )
        ending = piece_log[:, -1, :]
        weight_in = jnp.exp(ending[:, None, :] - piece_log) * piece_dt
        fresh_state = jnp.einsum(
            "rsh,rshp,rsn->rhpn", weight_in, piece_x, piece_b, precision=HIGHEST
        )
        carried = jnp.exp(ending)[:, :, None, None] * carried + fresh_state
        return (carried, inside + earlier)

    start_state = jnp.zeros((req_count, head_count, head_dim, state_dim), jnp.float32)
    final_state, outputs = lax.scan(
        advance,
        start_state,
        (shaped_x, shaped_dt, shaped_bs, shaped_cs, shaped_b, shaped_c, decays),
    )
    scanned = jnp.moveaxis(outputs, 0, 1).reshape(req_count, seq_len, head_count, head_dim)
    return (scanned + skip_gain[:, None] * head_in, final_state)


def body(
    tokens,
    lengths,
    gate_proj,
    input_proj,
    state_proj,
    step_proj,
    out_proj,
    conv_weight,
    step_bias,
    log_rate,
    skip_gain,
    norm_gain,
):
    unit_count = lax.axis_size("unit")
    unit_id = lax.axis_index("unit")
    group_reqs, seq_len, model_dim = tokens.shape
    own_reqs = group_reqs // unit_count
    inner_dim = gate_proj.shape[1]
    head_count = log_rate.shape[0]
    head_dim = inner_dim // head_count
    state_dim = state_proj.shape[1] // 2
    flat_tokens = tokens.reshape(group_reqs * seq_len, model_dim)
    rate_per = -jnp.exp(log_rate)
    position = jnp.arange(seq_len)
    moved = (
        lax.all_to_all(
            gate_proj.astype(jnp.bfloat16), "unit", split_axis=1, concat_axis=0, tiled=True
        ),
        lax.all_to_all(
            input_proj.astype(jnp.bfloat16), "unit", split_axis=1, concat_axis=0, tiled=True
        ),
        lax.all_to_all(
            state_proj.astype(jnp.bfloat16), "unit", split_axis=1, concat_axis=0, tiled=True
        ),
        lax.all_to_all(
            step_proj.astype(jnp.bfloat16), "unit", split_axis=1, concat_axis=0, tiled=True
        ),
        lax.all_to_all(
            out_proj.astype(jnp.bfloat16), "unit", split_axis=1, concat_axis=0, tiled=True
        ),
    )
    pieces = (
        lax.all_gather(moved[0], "req", axis=0, tiled=True),
        lax.all_gather(moved[1], "req", axis=0, tiled=True),
        lax.all_gather(moved[2], "req", axis=0, tiled=True),
        lax.all_gather(moved[3], "req", axis=0, tiled=True),
        lax.all_gather(moved[4], "req", axis=0, tiled=True),
    )
    projected = tuple(
        (
            jnp.dot(flat_tokens, weight_piece, preferred_element_type=jnp.float32)
            for weight_piece in pieces[:4]
        )
    )
    out_piece = pieces[4]
    gate_sum, input_sum, state_sum, step_sum, out_block = projected + (out_piece,)

    def as_cols(summed):
        return summed.astype(jnp.bfloat16).reshape(group_reqs, seq_len, summed.shape[1])

    gate_cols = as_cols(gate_sum)
    input_cols = as_cols(input_sum)
    state_cols = as_cols(state_sum)
    step_cols = as_cols(step_sum)
    own_len = lax.dynamic_slice_in_dim(lengths, unit_id * own_reqs, own_reqs, 0)
    own_live = (position[None, :] < own_len[:, None]).astype(jnp.float32)
    gate_all, input_all, state_all, step_all = (
        lax.all_to_all(gate_cols, "unit", split_axis=0, concat_axis=2, tiled=True),
        lax.all_to_all(input_cols, "unit", split_axis=0, concat_axis=2, tiled=True),
        lax.all_to_all(state_cols, "unit", split_axis=0, concat_axis=2, tiled=True),
        lax.all_to_all(step_cols, "unit", split_axis=0, concat_axis=2, tiled=True),
    )
    x_conv = causal_conv(input_all, conv_weight[:, :inner_dim])
    s_conv = causal_conv(state_all, conv_weight[:, inner_dim:])
    step_size = jax.nn.softplus(step_all.astype(jnp.float32) + step_bias) * own_live[..., None]
    scanned, final_state = ssd_scan(
        x_conv.reshape(own_reqs, seq_len, head_count, head_dim),
        step_size,
        s_conv[..., :state_dim],
        s_conv[..., state_dim:],
        rate_per,
        skip_gain,
        SPAN,
    )
    gated = scanned.reshape(own_reqs, seq_len, inner_dim) * jax.nn.silu(
        gate_all.astype(jnp.float32)
    )
    spread = jnp.mean(gated * gated, axis=-1, keepdims=True)
    normed = (gated * lax.rsqrt(spread + EPSILON) * norm_gain).astype(jnp.bfloat16)
    returned = lax.all_to_all(normed, "unit", split_axis=2, concat_axis=0, tiled=True)
    mixed = lax.psum_scatter(
        jnp.einsum("rse,de->rsd", returned, out_block, preferred_element_type=jnp.float32),
        "unit",
        scatter_dimension=0,
        tiled=True,
    )
    mixed_out = (mixed * own_live[..., None]).astype(jnp.bfloat16)
    return (mixed_out, final_state)


def solution(mesh):
    placed = (
        P("req", None, None),
        P("req"),
        P(("req", "unit"), None),
        P(("req", "unit"), None),
        P(("req", "unit"), None),
        P(("req", "unit"), None),
        P(("req", "unit"), None),
        P(),
        P(),
        P(),
        P(),
        P(),
    )
    return jax.shard_map(
        body,
        mesh=mesh,
        in_specs=placed,
        out_specs=(P(("req", "unit"), None, None), P(("req", "unit"), None, None, None)),
        check_vma=False,
    )
```

profile of v0, /device:TPU:1, one launch (start us, length us, event | category | flops | bytes accessed | tf_op | source)
XLA Modules:
  0.0 799.4 jit_solution(10832921844835051563)
XLA Ops:
  8.6 7.6 all-to-all-start
  28.2 6.7 all-to-all-start.4
  34.9 14.1 %all-gather = bf16[8,192,3]{1,2,0:T(4,128)(2,1)S(1)} all-gather(bf16[1,192,3]{1,2,0:T(4,128)(2,1)S(1)} %reshape.481), channel_id=1, replica_groups=mesh['req'=8,'unit'=16] {'req'}, dimensions={0}, use_global_device_ids=true | all-gather | bytes 10368 | tf_op jit(solution)/shard_map/all_gather | solution.py:121
  49.1 12.0 %convolution_convert_fusion.3 = bf16[6144,3]{0,1:T(4,128)(2,1)} fusion(bf16[6144,1536]{1,0:T(8,128)(2,1)} %bitcast.188, bf16[1536,3]{0,1:T(4,128)(2,1)S(1)} %reshape.482), kind=kOutput, calls=%fused_computation.50 | convolution fusion | flops 56641536 | bytes 18920448 | tf_op jit(solution)/shard_map/dot_general | solution.py:126
  61.1 6.9 all-to-all-start.1
  68.2 13.0 %all-gather.1 = bf16[8,192,16]{1,2,0:T(8,128)(2,1)S(1)} all-gather(bf16[1,192,16]{1,2,0:T(8,128)(2,1)S(1)} %reshape.483), channel_id=1, replica_groups=mesh['req'=8,'unit'=16] {'req'}, dimensions={0}, use_global_device_ids=true | all-gather | bytes 55296 | tf_op jit(solution)/shard_map/all_gather | solution.py:120
  81.4 11.3 %convolution_convert_fusion.2 = bf16[6144,16]{0,1:T(8,128)(2,1)S(1)} fusion(bf16[6144,1536]{1,0:T(8,128)(2,1)} %bitcast.189, bf16[1536,16]{0,1:T(8,128)(2,1)S(1)} %reshape.484), kind=kOutput, calls=%fused_computation.49 | convolution fusion | flops 302088192 | bytes 19120128 | tf_op jit(solution)/shard_map/dot_general | solution.py:126
  93.4 6.9 all-to-all-start.2
  101.8 5.3 all-to-all-done.2
  107.1 3.6 all-to-all-start.6
  110.7 14.9 %all_gather.16 = bf16[1536,192]{1,0:T(8,128)(2,1)S(1)} all-gather(bf16[192,192]{1,0:T(8,128)(2,1)S(1)} %all_to_all.119), channel_id=1, replica_groups=mesh['req'=8,'unit'=16] {'req'}, dimensions={0}, use_global_device_ids=true | all-gather | bytes 663552 | tf_op jit(solution)/shard_map/all_gather | solution.py:119
  125.6 6.9 all-to-all-start.5
  132.6 10.6 %convolution_convert_fusion.1 = bf16[6144,192]{0,1:T(8,128)(2,1)S(1)} fusion(bf16[6144,1536]{1,0:T(8,128)(2,1)} %bitcast.190, bf16[1536,192]{1,0:T(8,128)(2,1)S(1)} %all_gather.16), kind=kOutput, calls=%fused_computation.45 | convolution fusion | flops 3625058304 | bytes 21823488 | tf_op jit(solution)/shard_map/dot_general | solution.py:126
  145.1 6.9 all-to-all-start.3
  152.0 14.2 %all_gather.18 = bf16[1536,192]{1,0:T(8,128)(2,1)S(1)} all-gather(bf16[192,192]{1,0:T(8,128)(2,1)S(1)} %all_to_all.129), channel_id=1, replica_groups=mesh['req'=8,'unit'=16] {'req'}, dimensions={0}, use_global_device_ids=true | all-gather | bytes 663552 | tf_op jit(solution)/shard_map/all_gather | solution.py:118
  166.2 10.6 %convolution_convert_fusion = bf16[6144,192]{0,1:T(8,128)(2,1)S(1)} fusion(bf16[6144,1536]{1,0:T(8,128)(2,1)} %bitcast.191, bf16[1536,192]{1,0:T(8,128)(2,1)S(1)} %all_gather.18), kind=kOutput, calls=%fused_computation.44 | convolution fusion | flops 3625058304 | bytes 21823488 | tf_op jit(solution)/shard_map/dot_general | solution.py:126
  183.6 4.9 all-to-all-start.7
  192.8 6.9 divide_multiply_fusion
  199.6 8.0 transpose_reshape_reshape.3
  207.6 173.0 %while.13 = (s32[]{:T(128)}, f32[1,48,64,128]{3,2,1,0:T(8,128)S(1)}, f32[3,1,128,48,64]{2,0,4,3,1:T(4,128)}, f32[3,1,128,48]{2,3,1,0:T(8,128)S(1)}, f32[3,1,128,...) while((s32[]{:T(128)}, ...), condition=%wide.region_2.3_spmd.clone, body=%wide.region_1.2_spmd.clone.sunk | while | flops 1822060544 | bytes 19582040 | solution.py:66
  207.6 2.3 fusion.97
  210.0 4.5 constant_dynamic-slice_fusion.4
  216.3 7.4 bitcast_add_fusion.5
  223.7 39.1 %dynamic_update_slice.6 = f32[3,1,128,48,64]{2,0,4,3,1:T(4,128)} dynamic-update-slice(f32[3,1,128,48,64]{2,0,4,3,1:T(4,128)} %get-tuple-element.262, f32[1,1,128,48,64]{2,0,4,3,1:T(1,128)} %bitcast.194, s32[]{:T(128)} %get-tuple-element.260, s32[]{:T(128)} %constant.43.clone.1..sunk, s32[]{:T(128)} %constant.43.clone.1..sunk, s32[]{:T(128)} %constant.43.clone.1..sunk, s32[]{:T(128)} %constant.43.clone.1..sunk) | dynamic-update-slice | bytes 3145732 | tf_op jit(solution)/shard_map/while/body/jit(dynamic_update_index_in_dim)/dynamic_update_slice | solution.py:66
  263.1 2.2 bitcast_add_fusion.4
  265.3 2.3 fusion.97
  267.6 4.5 constant_dynamic-slice_fusion.4
  274.0 7.4 bitcast_add_fusion.5
  281.3 39.1 %dynamic_update_slice.6 = f32[3,1,128,48,64]{2,0,4,3,1:T(4,128)} dynamic-update-slice(f32[3,1,128,48,64]{2,0,4,3,1:T(4,128)} %get-tuple-element.262, f32[1,1,128,48,64]{2,0,4,3,1:T(1,128)} %bitcast.194, s32[]{:T(128)} %get-tuple-element.260, s32[]{:T(128)} %constant.43.clone.1..sunk, s32[]{:T(128)} %constant.43.clone.1..sunk, s32[]{:T(128)} %constant.43.clone.1..sunk, s32[]{:T(128)} %constant.43.clone.1..sunk) | dynamic-update-slice | bytes 3145732 | tf_op jit(solution)/shard_map/while/body/jit(dynamic_update_index_in_dim)/dynamic_update_slice | solution.py:66
  320.7 2.2 bitcast_add_fusion.4
  323.0 2.3 fusion.97
  325.3 4.5 constant_dynamic-slice_fusion.4
  331.6 7.4 bitcast_add_fusion.5
  339.0 39.1 %dynamic_update_slice.6 = f32[3,1,128,48,64]{2,0,4,3,1:T(4,128)} dynamic-update-slice(f32[3,1,128,48,64]{2,0,4,3,1:T(4,128)} %get-tuple-element.262, f32[1,1,128,48,64]{2,0,4,3,1:T(1,128)} %bitcast.194, s32[]{:T(128)} %get-tuple-element.260, s32[]{:T(128)} %constant.43.clone.1..sunk, s32[]{:T(128)} %constant.43.clone.1..sunk, s32[]{:T(128)} %constant.43.clone.1..sunk, s32[]{:T(128)} %constant.43.clone.1..sunk) | dynamic-update-slice | bytes 3145732 | tf_op jit(solution)/shard_map/while/body/jit(dynamic_update_index_in_dim)/dynamic_update_slice | solution.py:66
  380.6 9.1 %reshape_transpose.3 = f32[1,384,3072]{1,2,0:T(8,128)} reshape(f32[3,1,128,48,64]{2,0,4,3,1:T(4,128)} %get-tuple-element.60) | data formatting | bytes 9437184 | tf_op jit(solution)/shard_map/reshape;transpose | solution.py:71
  389.7 6.8 all-to-all-start.9
  396.5 15.3 %multiply_reduce_fusion = (f32[384]{0:T(512)S(1)}, f32[1,384,3072]{1,2,0:T(8,128)S(1)}) fusion(bf16[16,384,192]{1,2,0:T(8,128)(2,1)} %all-to-all-done.7, f32[1,384,3072]{1,2,0:T(8,128)} %reshape_transpose.3, f32[3072]{0:T(1024)S(1)} %mul.288, f32[1,384,3072]{1,2,0:T(8,128)} %bitcast.193, f32[3072]{0:T(1024)S(1)} %bitcast.216, f32[3072]{0:T(1024)S(1)} %bitcast.218, ...), kind=kLoop, calls=%fused_computation.64 | loop fusion | flops 24772224 | bytes 16578048 | tf_op jit(solution)/shard_map/reduce_sum | solution.py:163
  412.4 44.7 %copy.164 = bf16[1,384,3072]{1,0,2:T(2,128)(2,1)} copy(bf16[1,384,3072]{1,2,0:T(8,128)(2,1)S(1)} %multiply_convert_fusion) | data formatting | bytes 4718592 | tf_op jit(solution)/shard_map/convert_element_type | solution.py:164
  457.6 50.9 %reduce.4 = bf16[3072,384]{1,0:T(8,128)(2,1)S(1)} reduce(bf16[3072,1,384]{2,1,0:T(2,128)(2,1)} %bitcast.195, bf16[]{:T(256)} %broadcast.240), dimensions={1}, to_apply=%bitcast.159.reduce_sub_computation | reduce | bytes 4718594
  508.4 2.2 reshape.500
  510.6 6.8 all-to-all-start.8
  517.5 16.9 %all_gather.19 = bf16[1536,192]{1,0:T(8,128)(2,1)S(1)} all-gather(bf16[192,192]{1,0:T(8,128)(2,1)S(1)} %all_to_all.138), channel_id=1, replica_groups=mesh['req'=8,'unit'=16] {'req'}, dimensions={0}, use_global_device_ids=true | all-gather | bytes 663552 | tf_op jit(solution)/shard_map/all_gather | solution.py:122
  534.4 10.7 %all-to-all-done.8 = bf16[16,2,36864]{2,1,0:T(2,128)(2,1)S(1)} async-done(((bf16[16,2,36864]{2,1,0:T(2,128)(2,1)}), bf16[16,2,36864]{2,1,0:T(2,128)(2,1)S(1)}, u32[]{:S(2)}, u32[]{:S(2)}) %all-to-all-start.8) | async-done | bytes 2359328 | tf_op jit(solution)/shard_map/all_to_all | solution.py:165
  545.1 6.9 reshape.501
  552.1 2.7 copy.147
  554.8 14.9 %fusion.50 = f32[16,384,1536]{2,1,0:T(8,128)} fusion(bf16[16,384,192]{1,2,0:T(8,128)(2,1)S(1)} %bitcast.197, bf16[1536,192]{1,0:T(8,128)(2,1)S(1)} %all_gather.19), kind=kOutput, calls=%fused_computation.70 | convolution fusion | flops 3623878656 | bytes 40697856 | tf_op jit(solution)/shard_map/rse,de->rsd/dot_general | solution.py:167
  570.3 219.0 %reduce-scatter.4.cloned.1.call-done = f32[1,384,1536]{2,1,0:T(8,128)} async-done(((f32[16,384,1536]{2,1,0:T(8,128)}), f32[1,384,1536]{2,1,0:T(8,128)}) %reduce-scatter.4.cloned.1.call-update) | async-done | bytes 2359312
  789.3 2.9 multiply_convert_fusion.1
  (99 shorter events, 39.3 us)
Async XLA Ops:
  8.6 19.6 %all-to-all-start = ((bf16[12,16,3]{0,2,1:T(4,128)(2,1)}), bf16[12,16,3]{0,2,1:T(4,128)(2,1)S(1)}, u32[]{:S(2)}, u32[]{:S(2)}) async-start(bf16[12,16,3]{0,2,1:T(4,128)(2,1)} %all_to_all.111), calls=%async_computation | async-start | bytes 32768 | tf_op jit(solution)/shard_map/all_to_all | solution.py:110
  28.2 32.9 %all-to-all-start.4 = ((bf16[12,16,16]{0,2,1:T(8,128)(2,1)}), bf16[12,16,16]{0,2,1:T(8,128)(2,1)S(1)}, u32[]{:S(2)}, u32[]{:S(2)}) async-start(bf16[12,16,16]{0,2,1:T(8,128)(2,1)} %bitcast.17), calls=%async_computation.4 | async-start | bytes 131072 | tf_op jit(solution)/shard_map/all_to_all | solution.py:107
  61.1 32.3 %all-to-all-start.1 = ((bf16[16,384,3]{1,2,0:T(4,128)(2,1)}), bf16[16,384,3]{1,2,0:T(4,128)(2,1)S(1)}, u32[]{:S(2)}, u32[]{:S(2)}) async-start(bf16[16,384,3]{1,2,0:T(4,128)(2,1)} %bitcast.2), calls=%async_computation.1 | async-start | bytes 98304 | tf_op jit(solution)/shard_map/all_to_all | solution.py:146
  81.4 19.1 %copy-start.3 = (f32[48]{0:T(128)S(1)}, f32[48]{0:T(128)}, u32[]{:S(2)}) copy-start(f32[48]{0:T(128)} %param.22) | copy-start | bytes 580
  93.4 13.7 %all-to-all-start.2 = ((bf16[12,16,192]{2,0,1:T(8,128)(2,1)}), bf16[12,16,192]{2,0,1:T(8,128)(2,1)S(1)}, u32[]{:S(2)}, u32[]{:S(2)}) async-start(bf16[12,16,192]{2,0,1:T(8,128)(2,1)} %copy.121), calls=%async_computation.2 | async-start | bytes 262144 | tf_op jit(solution)/shard_map/all_to_all | solution.py:104
  107.1 18.5 %all-to-all-start.6 = ((bf16[12,16,192]{2,0,1:T(8,128)(2,1)}), bf16[12,16,192]{2,0,1:T(8,128)(2,1)S(1)}, u32[]{:S(2)}, u32[]{:S(2)}) async-start(bf16[12,16,192]{2,0,1:T(8,128)(2,1)} %copy.139), calls=%async_computation.6 | async-start | bytes 262144 | tf_op jit(solution)/shard_map/all_to_all | solution.py:101
  125.6 19.4 %all-to-all-start.5 = ((bf16[16,384,16]{1,2,0:T(8,128)(2,1)}), bf16[16,384,16]{1,2,0:T(8,128)(2,1)S(1)}, u32[]{:S(2)}, u32[]{:S(2)}) async-start(bf16[16,384,16]{1,2,0:T(8,128)(2,1)} %bitcast.158), calls=%async_computation.5 | async-start | bytes 393216 | tf_op jit(solution)/shard_map/all_to_all | solution.py:145
  145.1 38.5 %all-to-all-start.3 = ((bf16[16,384,192]{1,2,0:T(8,128)(2,1)}), bf16[16,384,192]{1,2,0:T(8,128)(2,1)}, u32[]{:S(2)}, u32[]{:S(2)}) async-start(bf16[16,384,192]{1,2,0:T(8,128)(2,1)} %bitcast.199), calls=%async_computation.3 | async-start | bytes 4718592 | tf_op jit(solution)/shard_map/all_to_all | solution.py:144
  183.6 206.1 %all-to-all-start.7 = ((bf16[16,384,192]{1,2,0:T(8,128)(2,1)}), bf16[16,384,192]{1,2,0:T(8,128)(2,1)}, u32[]{:S(2)}, u32[]{:S(2)}) async-start(bf16[16,384,192]{1,2,0:T(8,128)(2,1)} %bitcast.198), calls=%async_computation.7 | async-start | bytes 4718592 | tf_op jit(solution)/shard_map/all_to_all | solution.py:143
  190.7 2.1 copy-start.1
  380.6 9.1 %copy-start = (f32[1,48,64,128]{3,2,1,0:T(8,128)}, f32[1,48,64,128]{3,2,1,0:T(8,128)S(1)}, u32[]{:S(2)}) copy-start(f32[1,48,64,128]{3,2,1,0:T(8,128)S(1)} %get-tuple-element.59) | copy-start | bytes 4718596
  389.7 120.9 %all-to-all-start.9 = ((bf16[12,16,192]{2,0,1:T(8,128)(2,1)}), bf16[12,16,192]{2,0,1:T(8,128)(2,1)S(1)}, u32[]{:S(2)}, u32[]{:S(2)}) async-start(bf16[12,16,192]{2,0,1:T(8,128)(2,1)} %copy.142), calls=%async_computation.9 | async-start | bytes 262144 | tf_op jit(solution)/shard_map/all_to_all | solution.py:113
  396.5 15.3 %copy-start.2 = (f32[3072]{0:T(1024)S(1)}, f32[3072]{0:T(1024)}, u32[]{:S(2)}) copy-start(f32[3072]{0:T(1024)} %param.25) | copy-start | bytes 36868
  510.6 34.5 %all-to-all-start.8 = ((bf16[16,2,36864]{2,1,0:T(2,128)(2,1)}), bf16[16,2,36864]{2,1,0:T(2,128)(2,1)S(1)}, u32[]{:S(2)}, u32[]{:S(2)}) async-start(bf16[16,2,36864]{2,1,0:T(2,128)(2,1)} %reshape.500), calls=%async_computation.8 | async-start | bytes 4718592 | tf_op jit(solution)/shard_map/all_to_all | solution.py:165
  517.4 271.9 %reduce-scatter.4.cloned.1.call-start = ((), (), s32[]{:S(2)}) async-start(), calls=%async_computation.11 | async-start | bytes 40108032
Sparse Core Ops, SparseCore 0:
  569.9 219.3 reduce-scatter.3
where the time goes:
time: 813 us; the launch traced here: 799 us
  waiting for transfers between devices  237 us (29%)
  local copies, waits for them, and re-layouts  226 us (28%)
  matrix products  97.7 us (12%)
  other arithmetic  86.6 us (11%)
  blocking collectives  73.2 us (9%)
  starting transfers between devices  64 us (8%)
  between operations  14.8 us (2%)
    unnamed x2, waiting for transfers between devices  219 us
    dynamic_update_slice x3, local copies, waits for them, and re-layouts, ssd_scan(): lax.scan(advance, start_state, (shaped_x, shaped_dt, shaped_bs, shaped_cs...  117 us
    unnamed x2, other arithmetic  50.9 us
    convert_element_type x1, local copies, waits for them, and re-layouts, body(): (gated * lax.rsqrt(spread + EPSILON) * norm_gain).astype(jnp.bfloat16)  44.7 us
    dot_general x4, matrix products, body(): jnp.dot(flat_tokens, weight_piece, preferred_element_type=jnp.float32)  44.5 us
    dot_general x3, matrix products, advance(): inside = jnp.einsum('rtsh,rshp->rthp', mixing, piece_x, precision=HIGHEST)  22.1 us
    all_gather x1, blocking collectives, body(): lax.all_gather(moved[4], 'req', axis=0, tiled=True)  16.9 us
  transfers between devices with their start and end apart: 11, of which 4 were waited for; matrix products, arithmetic and copies ran while one was open for 47% of the time, Pallas kernels for 0%

commit v1 on v0

--- a/solution.py
+++ b/solution.py
@@ -162,7 +162,10 @@
     )
     spread = jnp.mean(gated * gated, axis=-1, keepdims=True)
     normed = (gated * lax.rsqrt(spread + EPSILON) * norm_gain).astype(jnp.bfloat16)
-    returned = lax.all_to_all(normed, "unit", split_axis=2, concat_axis=0, tiled=True)
+    size = lax.axis_size("unit")
+    tiles = jnp.stack(jnp.split(normed, size, axis=2), axis=0)
+    tiles = lax.all_to_all(tiles, "unit", split_axis=0, concat_axis=0)
+    returned = jnp.concatenate(tiles, axis=0)
     mixed = lax.psum_scatter(
         jnp.einsum("rse,de->rsd", returned, out_block, preferred_element_type=jnp.float32),
         "unit",

time: 813 us -> 729 us (0.90)
  other arithmetic: 86.6 us -> 35.9 us
  local copies, waits for them, and re-layouts: 226 us -> 180 us
  starting transfers between devices: 64 us -> 75.7 us
    unnamed x2 -> x1, other arithmetic: 50.9 us -> 0.01 us
    convert_element_type x1 -> x0, local copies, waits for them, and re-layouts: 44.7 us -> none  [body(): (gated * lax.rsqrt(spread + EPSILON) * norm_gain).astype(jnp.bfloat16)]
    all_to_all x1, starting transfers between devices: 6.88 us -> 19 us  [body(): lax.all_to_all(input_cols, 'unit', split_axis=0, concat_axis=2, tiled=True)]
  transfers between devices with their start and end apart: 11 -> 11, of which waited for: 4 -> 4; matrix products, arithmetic and copies ran while one was open for 47% -> 41% of each run, Pallas kernels for 0% -> 0%
where the time goes in v1:
time: 729 us; the launch traced here: 716 us
  waiting for transfers between devices  237 us (33%)
  local copies, waits for them, and re-layouts  180 us (25%)
  matrix products  99.1 us (14%)
  starting transfers between devices  75.7 us (10%)
  blocking collectives  73.3 us (10%)
  other arithmetic  35.9 us (5%)
  between operations  14.7 us (2%)
    unnamed x2, waiting for transfers between devices  219 us
    dynamic_update_slice x3, local copies, waits for them, and re-layouts, ssd_scan(): lax.scan(advance, start_state, (shaped_x, shaped_dt, shaped_bs, shaped_cs...  117 us
    dot_general x4, matrix products, body(): jnp.dot(flat_tokens, weight_piece, preferred_element_type=jnp.float32)  44.2 us
    dot_general x3, matrix products, advance(): inside = jnp.einsum('rtsh,rshp->rthp', mixing, piece_x, precision=HIGHEST)  22.1 us
    all_to_all x1, starting transfers between devices, body(): lax.all_to_all(input_cols, 'unit', split_axis=0, concat_axis=2, tiled=True)  19 us
    all_gather x1, blocking collectives, body(): lax.all_gather(moved[4], 'req', axis=0, tiled=True)  17 us
    dot_general x1, matrix products, body(): jnp.einsum('rse,de->rsd', returned, out_block, preferred_element_type=jnp...  16.6 us
    dynamic_slice x6, local copies, waits for them, and re-layouts, ssd_scan(): lax.scan(advance, start_state, (shaped_x, shaped_dt, shaped_bs, shaped_cs...  16.2 us
  transfers between devices with their start and end apart: 11, of which 4 were waited for; matrix products, arithmetic and copies ran while one was open for 41% of the time, Pallas kernels for 0%

profile of v1, /device:TPU:1, one launch (start us, length us, event | category | flops | bytes accessed | tf_op | source)
XLA Modules:
  0.0 715.7 jit_solution(15686566084161690954)
XLA Ops:
  8.6 7.6 %all-to-all-start = ((bf16[12,16,3]{0,2,1:T(4,128)(2,1)}), bf16[12,16,3]{0,2,1:T(4,128)(2,1)S(1)}, u32[]{:S(2)}, u32[]{:S(2)}) async-start(bf16[12,16,3]{0,2,1:T(4,128)(2,1)} %all_to_all.101), calls=%async_computation | async-start | bytes 32768 | tf_op jit(solution)/shard_map/all_to_all | solution.py:110
  28.3 6.7 all-to-all-start.4
  35.0 14.1 %all-gather = bf16[8,192,3]{1,2,0:T(4,128)(2,1)S(1)} all-gather(bf16[1,192,3]{1,2,0:T(4,128)(2,1)S(1)} %reshape.485), channel_id=1, replica_groups=mesh['req'=8,'unit'=16] {'req'}, dimensions={0}, use_global_device_ids=true | all-gather | bytes 10368 | tf_op jit(solution)/shard_map/all_gather | solution.py:121
  49.2 12.0 %convolution_convert_fusion.3 = bf16[6144,3]{0,1:T(4,128)(2,1)} fusion(bf16[6144,1536]{1,0:T(8,128)(2,1)} %bitcast.245, bf16[1536,3]{0,1:T(4,128)(2,1)S(1)} %reshape.486), kind=kOutput, calls=%fused_computation.50 | convolution fusion | flops 56641536 | bytes 18920448 | tf_op jit(solution)/shard_map/dot_general | solution.py:126
  61.2 6.9 all-to-all-start.1
  68.3 13.0 %all-gather.1 = bf16[8,192,16]{1,2,0:T(8,128)(2,1)S(1)} all-gather(bf16[1,192,16]{1,2,0:T(8,128)(2,1)S(1)} %reshape.487), channel_id=1, replica_groups=mesh['req'=8,'unit'=16] {'req'}, dimensions={0}, use_global_device_ids=true | all-gather | bytes 55296 | tf_op jit(solution)/shard_map/all_gather | solution.py:120
  81.5 11.3 %convolution_convert_fusion.2 = bf16[6144,16]{0,1:T(8,128)(2,1)S(1)} fusion(bf16[6144,1536]{1,0:T(8,128)(2,1)} %bitcast.246, bf16[1536,16]{0,1:T(8,128)(2,1)S(1)} %reshape.488), kind=kOutput, calls=%fused_computation.49 | convolution fusion | flops 302088192 | bytes 19120128 | tf_op jit(solution)/shard_map/dot_general | solution.py:126
  93.5 6.9 all-to-all-start.2
  101.9 5.3 all-to-all-done.2
  107.2 3.6 all-to-all-start.6
  110.8 14.9 %all_gather.16 = bf16[1536,192]{1,0:T(8,128)(2,1)S(1)} all-gather(bf16[192,192]{1,0:T(8,128)(2,1)S(1)} %all_to_all.109), channel_id=1, replica_groups=mesh['req'=8,'unit'=16] {'req'}, dimensions={0}, use_global_device_ids=true | all-gather | bytes 663552 | tf_op jit(solution)/shard_map/all_gather | solution.py:119
  125.8 6.9 all-to-all-start.5
  132.7 10.5 %convolution_convert_fusion.1 = bf16[6144,192]{0,1:T(8,128)(2,1)S(1)} fusion(bf16[6144,1536]{1,0:T(8,128)(2,1)} %bitcast.247, bf16[1536,192]{1,0:T(8,128)(2,1)S(1)} %all_gather.16), kind=kOutput, calls=%fused_computation.45 | convolution fusion | flops 3625058304 | bytes 21823488 | tf_op jit(solution)/shard_map/dot_general | solution.py:126
  143.2 1.8 copy.194
  145.1 19.0 %all-to-all-start.3 = ((bf16[16,384,192]{1,2,0:T(8,128)(2,1)}), bf16[16,384,192]{1,2,0:T(8,128)(2,1)}, u32[]{:S(2)}, u32[]{:S(2)}) async-start(bf16[16,384,192]{1,2,0:T(8,128)(2,1)} %bitcast.253), calls=%async_computation.3 | async-start | bytes 4718592 | tf_op jit(solution)/shard_map/all_to_all | solution.py:144
  164.1 14.2 %all_gather.18 = bf16[1536,192]{1,0:T(8,128)(2,1)S(1)} all-gather(bf16[192,192]{1,0:T(8,128)(2,1)S(1)} %all_to_all.119), channel_id=1, replica_groups=mesh['req'=8,'unit'=16] {'req'}, dimensions={0}, use_global_device_ids=true | all-gather | bytes 663552 | tf_op jit(solution)/shard_map/all_gather | solution.py:118
  178.3 10.5 %convolution_convert_fusion = bf16[6144,192]{0,1:T(8,128)(2,1)S(1)} fusion(bf16[6144,1536]{1,0:T(8,128)(2,1)} %bitcast.248, bf16[1536,192]{1,0:T(8,128)(2,1)S(1)} %all_gather.18), kind=kOutput, calls=%fused_computation.44 | convolution fusion | flops 3625058304 | bytes 21823488 | tf_op jit(solution)/shard_map/dot_general | solution.py:126
  193.6 2.1 all-to-all-done.3
  195.7 4.8 all-to-all-start.7
  200.5 2.1 bitcast_convert_fusion
  202.7 2.1 copy-done.1
  204.7 6.9 divide_multiply_fusion
  211.6 8.0 %transpose_reshape_reshape.3 = f32[3,1,128,48,64]{2,0,4,3,1:T(4,128)} reshape(f32[1,384,3072]{1,2,0:T(8,128)} %divide_multiply_fusion) | data formatting | bytes 9437184 | tf_op jit(solution)/shard_map/transpose;reshape;reshape | solution.py:33
  219.6 173.0 %while.13 = (s32[]{:T(128)}, f32[1,48,64,128]{3,2,1,0:T(8,128)S(1)}, f32[3,1,128,48,64]{2,0,4,3,1:T(4,128)}, f32[3,1,128,48]{2,3,1,0:T(8,128)S(1)}, f32[3,1,128,...) while((s32[]{:T(128)}, ...), condition=%wide.region_2.3_spmd.clone, body=%wide.region_1.2_spmd.clone.sunk | while | flops 1822060544 | bytes 19582040 | solution.py:66
  219.6 2.3 fusion.113
  222.0 4.5 constant_dynamic-slice_fusion.4
  228.3 7.4 %bitcast_add_fusion.5 = f32[1,128,48,64]{1,3,2,0:T(8,128)} fusion(f32[128,48,64]{0,2,1:T(8,128)S(1)} %fusion.113, f32[128,48,64]{0,2,1:T(8,128)S(1)} %bitcast.243, f32[128,48]{0,1:T(8,128)S(1)} %bitcast.254, f32[128,48]{0,1:T(8,128)S(1)} %get-tuple-element.246, f32[128,128]{1,0:T(8,128)S(1)} %fusion.114, ...), kind=kOutput, calls=%fused_computation.7.clone.1 | convolution fusion | flops 607911936 | bytes 4874240 | tf_op jit(solution)/shard_map/while/body/eval_jaxpr/rtsh,rshp->rthp/dot_general | solution.py:52
  235.7 39.1 %dynamic_update_slice.6 = f32[3,1,128,48,64]{2,0,4,3,1:T(4,128)} dynamic-update-slice(f32[3,1,128,48,64]{2,0,4,3,1:T(4,128)} %get-tuple-element.262, f32[1,1,128,48,64]{2,0,4,3,1:T(1,128)} %bitcast.251, s32[]{:T(128)} %get-tuple-element.260, s32[]{:T(128)} %constant.43.clone.1..sunk, s32[]{:T(128)} %constant.43.clone.1..sunk, s32[]{:T(128)} %constant.43.clone.1..sunk, s32[]{:T(128)} %constant.43.clone.1..sunk) | dynamic-update-slice | bytes 3145732 | tf_op jit(solution)/shard_map/while/body/jit(dynamic_update_index_in_dim)/dynamic_update_slice | solution.py:66
  275.1 2.2 bitcast_add_fusion.4
  277.3 2.3 fusion.113
  279.6 4.5 constant_dynamic-slice_fusion.4
  286.0 7.4 %bitcast_add_fusion.5 = f32[1,128,48,64]{1,3,2,0:T(8,128)} fusion(f32[128,48,64]{0,2,1:T(8,128)S(1)} %fusion.113, f32[128,48,64]{0,2,1:T(8,128)S(1)} %bitcast.243, f32[128,48]{0,1:T(8,128)S(1)} %bitcast.254, f32[128,48]{0,1:T(8,128)S(1)} %get-tuple-element.246, f32[128,128]{1,0:T(8,128)S(1)} %fusion.114, ...), kind=kOutput, calls=%fused_computation.7.clone.1 | convolution fusion | flops 607911936 | bytes 4874240 | tf_op jit(solution)/shard_map/while/body/eval_jaxpr/rtsh,rshp->rthp/dot_general | solution.py:52
  293.3 39.1 %dynamic_update_slice.6 = f32[3,1,128,48,64]{2,0,4,3,1:T(4,128)} dynamic-update-slice(f32[3,1,128,48,64]{2,0,4,3,1:T(4,128)} %get-tuple-element.262, f32[1,1,128,48,64]{2,0,4,3,1:T(1,128)} %bitcast.251, s32[]{:T(128)} %get-tuple-element.260, s32[]{:T(128)} %constant.43.clone.1..sunk, s32[]{:T(128)} %constant.43.clone.1..sunk, s32[]{:T(128)} %constant.43.clone.1..sunk, s32[]{:T(128)} %constant.43.clone.1..sunk) | dynamic-update-slice | bytes 3145732 | tf_op jit(solution)/shard_map/while/body/jit(dynamic_update_index_in_dim)/dynamic_update_slice | solution.py:66
  332.7 2.2 bitcast_add_fusion.4
  335.0 2.3 fusion.113
  337.3 4.5 constant_dynamic-slice_fusion.4
  343.6 7.4 %bitcast_add_fusion.5 = f32[1,128,48,64]{1,3,2,0:T(8,128)} fusion(f32[128,48,64]{0,2,1:T(8,128)S(1)} %fusion.113, f32[128,48,64]{0,2,1:T(8,128)S(1)} %bitcast.243, f32[128,48]{0,1:T(8,128)S(1)} %bitcast.254, f32[128,48]{0,1:T(8,128)S(1)} %get-tuple-element.246, f32[128,128]{1,0:T(8,128)S(1)} %fusion.114, ...), kind=kOutput, calls=%fused_computation.7.clone.1 | convolution fusion | flops 607911936 | bytes 4874240 | tf_op jit(solution)/shard_map/while/body/eval_jaxpr/rtsh,rshp->rthp/dot_general | solution.py:52
  351.0 39.1 %dynamic_update_slice.6 = f32[3,1,128,48,64]{2,0,4,3,1:T(4,128)} dynamic-update-slice(f32[3,1,128,48,64]{2,0,4,3,1:T(4,128)} %get-tuple-element.262, f32[1,1,128,48,64]{2,0,4,3,1:T(1,128)} %bitcast.251, s32[]{:T(128)} %get-tuple-element.260, s32[]{:T(128)} %constant.43.clone.1..sunk, s32[]{:T(128)} %constant.43.clone.1..sunk, s32[]{:T(128)} %constant.43.clone.1..sunk, s32[]{:T(128)} %constant.43.clone.1..sunk) | dynamic-update-slice | bytes 3145732 | tf_op jit(solution)/shard_map/while/body/jit(dynamic_update_index_in_dim)/dynamic_update_slice | solution.py:66
  390.4 2.2 bitcast_add_fusion.4
  392.6 9.1 %reshape_transpose.3 = f32[1,384,3072]{1,2,0:T(8,128)} reshape(f32[3,1,128,48,64]{2,0,4,3,1:T(4,128)} %get-tuple-element.60) | data formatting | bytes 9437184 | tf_op jit(solution)/shard_map/reshape;transpose | solution.py:71
  401.7 6.6 all-to-all-start.9
  408.4 15.3 %multiply_reduce_fusion = (f32[384]{0:T(512)S(1)}, f32[1,384,3072]{1,2,0:T(8,128)S(1)}) fusion(bf16[16,384,192]{1,2,0:T(8,128)(2,1)} %all-to-all-done.7, f32[1,384,3072]{1,2,0:T(8,128)} %reshape_transpose.3, f32[3072]{0:T(1024)S(1)} %mul.288, f32[1,384,3072]{1,2,0:T(8,128)} %bitcast.250, f32[3072]{0:T(1024)S(1)} %bitcast.270, f32[3072]{0:T(1024)S(1)} %bitcast.272, ...), kind=kLoop, calls=%fused_computation.64 | loop fusion | flops 24772224 | bytes 16578048 | tf_op jit(solution)/shard_map/reduce_sum | solution.py:163
  435.0 6.7 all-to-all-start.8
  441.8 17.0 %all_gather.19 = bf16[1536,192]{1,0:T(8,128)(2,1)S(1)} all-gather(bf16[192,192]{1,0:T(8,128)(2,1)S(1)} %all_to_all.125), channel_id=1, replica_groups=mesh['req'=8,'unit'=16] {'req'}, dimensions={0}, use_global_device_ids=true | all-gather | bytes 663552 | tf_op jit(solution)/shard_map/all_gather | solution.py:122
  458.8 10.6 %all-to-all-done.8 = bf16[16,1,384,192]{2,3,1,0:T(8,128)(2,1)} async-done(((bf16[16,1,384,192]{2,3,1,0:T(8,128)(2,1)}), bf16[16,1,384,192]{2,3,1,0:T(8,128)(2,1)}, u32[]{:S(2)}, u32[]{:S(2)}) %all-to-all-start.8) | async-done | bytes 2359328 | tf_op jit(solution)/shard_map/all_to_all | solution.py:167
  469.4 16.6 %fusion.50 = f32[16,384,1536]{2,1,0:T(8,128)} fusion(bf16[16,1,384,192]{2,3,1,0:T(8,128)(2,1)} %all-to-all-done.8, bf16[1536,192]{1,0:T(8,128)(2,1)S(1)} %all_gather.19), kind=kOutput, calls=%fused_computation.68 | convolution fusion | flops 3623878656 | bytes 40697856 | tf_op jit(solution)/shard_map/rse,de->rsd/dot_general | solution.py:170
  486.7 219.0 %reduce-scatter.4.cloned.1.call-done = f32[1,384,1536]{2,1,0:T(8,128)} async-done(((f32[16,384,1536]{2,1,0:T(8,128)}), f32[1,384,1536]{2,1,0:T(8,128)}) %reduce-scatter.4.cloned.1.call-update) | async-done | bytes 2359312
  705.6 2.9 multiply_convert_fusion.1
  (109 shorter events, 39.4 us)
Async XLA Ops:
  8.6 19.7 %all-to-all-start = ((bf16[12,16,3]{0,2,1:T(4,128)(2,1)}), bf16[12,16,3]{0,2,1:T(4,128)(2,1)S(1)}, u32[]{:S(2)}, u32[]{:S(2)}) async-start(bf16[12,16,3]{0,2,1:T(4,128)(2,1)} %all_to_all.101), calls=%async_computation | async-start | bytes 32768 | tf_op jit(solution)/shard_map/all_to_all | solution.py:110
  28.3 32.9 %all-to-all-start.4 = ((bf16[12,16,16]{0,2,1:T(8,128)(2,1)}), bf16[12,16,16]{0,2,1:T(8,128)(2,1)S(1)}, u32[]{:S(2)}, u32[]{:S(2)}) async-start(bf16[12,16,16]{0,2,1:T(8,128)(2,1)} %bitcast.17), calls=%async_computation.4 | async-start | bytes 131072 | tf_op jit(solution)/shard_map/all_to_all | solution.py:107
  61.2 32.3 %all-to-all-start.1 = ((bf16[16,384,3]{1,2,0:T(4,128)(2,1)}), bf16[16,384,3]{1,2,0:T(4,128)(2,1)S(1)}, u32[]{:S(2)}, u32[]{:S(2)}) async-start(bf16[16,384,3]{1,2,0:T(4,128)(2,1)} %bitcast.2), calls=%async_computation.1 | async-start | bytes 98304 | tf_op jit(solution)/shard_map/all_to_all | solution.py:146
  81.5 19.1 %copy-start.3 = (f32[48]{0:T(128)S(1)}, f32[48]{0:T(128)}, u32[]{:S(2)}) copy-start(f32[48]{0:T(128)} %param.22) | copy-start | bytes 580
  93.5 13.7 %all-to-all-start.2 = ((bf16[12,16,192]{2,0,1:T(8,128)(2,1)}), bf16[12,16,192]{2,0,1:T(8,128)(2,1)S(1)}, u32[]{:S(2)}, u32[]{:S(2)}) async-start(bf16[12,16,192]{2,0,1:T(8,128)(2,1)} %copy.156), calls=%async_computation.2 | async-start | bytes 262144 | tf_op jit(solution)/shard_map/all_to_all | solution.py:104
  107.2 18.5 %all-to-all-start.6 = ((bf16[12,16,192]{2,0,1:T(8,128)(2,1)}), bf16[12,16,192]{2,0,1:T(8,128)(2,1)S(1)}, u32[]{:S(2)}, u32[]{:S(2)}) async-start(bf16[12,16,192]{2,0,1:T(8,128)(2,1)} %copy.174), calls=%async_computation.6 | async-start | bytes 262144 | tf_op jit(solution)/shard_map/all_to_all | solution.py:101
  125.8 19.3 %all-to-all-start.5 = ((bf16[16,384,16]{1,2,0:T(8,128)(2,1)}), bf16[16,384,16]{1,2,0:T(8,128)(2,1)S(1)}, u32[]{:S(2)}, u32[]{:S(2)}) async-start(bf16[16,384,16]{1,2,0:T(8,128)(2,1)} %bitcast.216), calls=%async_computation.5 | async-start | bytes 393216 | tf_op jit(solution)/shard_map/all_to_all | solution.py:145
  145.1 50.6 %all-to-all-start.3 = ((bf16[16,384,192]{1,2,0:T(8,128)(2,1)}), bf16[16,384,192]{1,2,0:T(8,128)(2,1)}, u32[]{:S(2)}, u32[]{:S(2)}) async-start(bf16[16,384,192]{1,2,0:T(8,128)(2,1)} %bitcast.253), calls=%async_computation.3 | async-start | bytes 4718592 | tf_op jit(solution)/shard_map/all_to_all | solution.py:144
  195.7 206.0 %all-to-all-start.7 = ((bf16[16,384,192]{1,2,0:T(8,128)(2,1)}), bf16[16,384,192]{1,2,0:T(8,128)(2,1)}, u32[]{:S(2)}, u32[]{:S(2)}) async-start(bf16[16,384,192]{1,2,0:T(8,128)(2,1)} %bitcast.252), calls=%async_computation.7 | async-start | bytes 4718592 | tf_op jit(solution)/shard_map/all_to_all | solution.py:143
  202.6 2.1 copy-start.1
  392.6 9.1 %copy-start = (f32[1,48,64,128]{3,2,1,0:T(8,128)}, f32[1,48,64,128]{3,2,1,0:T(8,128)S(1)}, u32[]{:S(2)}) copy-start(f32[1,48,64,128]{3,2,1,0:T(8,128)S(1)} %get-tuple-element.59) | copy-start | bytes 4718596
  401.7 33.3 %all-to-all-start.9 = ((bf16[12,16,192]{2,0,1:T(8,128)(2,1)}), bf16[12,16,192]{2,0,1:T(8,128)(2,1)S(1)}, u32[]{:S(2)}, u32[]{:S(2)}) async-start(bf16[12,16,192]{2,0,1:T(8,128)(2,1)} %copy.176), calls=%async_computation.9 | async-start | bytes 262144 | tf_op jit(solution)/shard_map/all_to_all | solution.py:113
  408.3 15.3 %copy-start.2 = (f32[3072]{0:T(1024)S(1)}, f32[3072]{0:T(1024)}, u32[]{:S(2)}) copy-start(f32[3072]{0:T(1024)} %param.25) | copy-start | bytes 36868
  435.0 34.5 %all-to-all-start.8 = ((bf16[16,1,384,192]{2,3,1,0:T(8,128)(2,1)}), bf16[16,1,384,192]{2,3,1,0:T(8,128)(2,1)}, u32[]{:S(2)}, u32[]{:S(2)}) async-start(bf16[16,1,384,192]{2,3,1,0:T(8,128)(2,1)} %fusion.59), calls=%async_computation.8 | async-start | bytes 4718592 | tf_op jit(solution)/shard_map/all_to_all | solution.py:167
  441.7 264.0 %reduce-scatter.4.cloned.1.call-start = ((), (), s32[]{:S(2)}) async-start(), calls=%async_computation.11 | async-start | bytes 40108032
Sparse Core Ops, SparseCore 0:
  486.1 219.4 reduce-scatter.3
